TPU v7x, 32 devices: a whole 2x2x4 slice. The times are simulated.
32 devices in a mesh: dp: 8 (over y, x, core), mp: 4 (over z).
Axes of the slice: x: 2, y: 2, z: 4, core: 2. Of those that a mesh axis runs over, the one named last changes fastest.
Arguments:
- layer_input: bfloat16 [6464, 768], P(('dp', 'mp')), may hold values from -6 to 6
- lengths: int32 [32], P('dp'), may hold values from 10 to 202, as said below
- ln1_gain: float32 [768], replicated, may hold values from 0.5 to 1.5
- ln1_bias: float32 [768], replicated, may hold values from -1.25 to 1.25
- w_qkv: bfloat16 [768, 2304], P(None, 'mp'), may hold values from -0.21875 to 0.21875
- b_qkv: float32 [2304], P('mp'), may hold values from -1.25 to 1.25
- features: float32 [12, 64, 32], P('mp'), may hold values from -6 to 6
- w_out: bfloat16 [768, 768], P('mp'), may hold values from -1.75 to 1.75
- b_out: float32 [768], replicated, may hold values from -1.25 to 1.25
- ln2_gain: float32 [768], replicated, may hold values from 0.5 to 1.5
- ln2_bias: float32 [768], replicated, may hold values from -1.25 to 1.25
- w_up: bfloat16 [768, 3072], P(None, 'mp'), may hold values from -0.21875 to 0.21875
- b_up: float32 [3072], P('mp'), may hold values from -1.25 to 1.25
- w_down: bfloat16 [3072, 768], P('mp'), may hold values from -0.109375 to 0.109375
- b_down: float32 [768], replicated, may hold values from -1.25 to 1.25
- cotangent: bfloat16 [6464, 768], P(('dp', 'mp')), may hold values from -6 to 6
Outputs:
- layer_output: bfloat16 [6464, 768], P(('dp', 'mp'))
- grad_x: float32 [6464, 768], P(('dp', 'mp'))
- grad_ln1_gain: float32 [768], replicated
- grad_ln1_bias: float32 [768], replicated
- grad_w_qkv: float32 [768, 2304], P('dp', 'mp')
- grad_b_qkv: float32 [2304], P('mp')
- grad_w_out: float32 [768, 768], P('mp', 'dp')
- grad_b_out: float32 [768], replicated
- grad_ln2_gain: float32 [768], replicated
- grad_ln2_bias: float32 [768], replicated
- grad_w_up: float32 [768, 3072], P('dp', 'mp')
- grad_b_up: float32 [3072], P('mp')
- grad_w_down: float32 [3072, 768], P('mp', 'dp')
- grad_b_down: float32 [768], replicated
Inputs may be any that keep to these rules, and one draw needn't show every extreme that they name: A molecule's live tokens are the first lengths[m] of its 202 slots; some molecule has exactly 202 and some exactly 10.
All inputs are finite; a program needn't handle non-finite values.
Results may differ from a plain program's by a relative error of at most 0.02.
Values may be sent and summed in bfloat16 or wider, within the bound.
A program may use at most 128 MiB of HBM per device.

v0:
```python
import jax
import jax.numpy as jnp
from jax import lax
from jax.sharding import PartitionSpec as P

MAXLEN = 202
EPSILON = 1e-05


def norm_rows(values, gain, shift):
    centred = values - jnp.mean(values, axis=-1, keepdims=True)
    factor = lax.rsqrt(jnp.mean(centred * centred, axis=-1, keepdims=True) + EPSILON)
    normed = centred * factor
    return (normed * gain + shift, normed, factor)


def norm_back(grad_norm, normed, factor, gain):
    grad_hat = grad_norm * gain
    inner = (
        grad_hat
        - jnp.mean(grad_hat, axis=-1, keepdims=True)
        - normed * jnp.mean(grad_hat * normed, axis=-1, keepdims=True)
    )
    return (factor * inner, jnp.sum(grad_norm * normed, axis=0), jnp.sum(grad_norm, axis=0))


def rotate(values, positions):
    half = values.shape[-1] // 2
    freq = 10000.0 ** (-jnp.arange(half, dtype=jnp.float32) * 2.0 / values.shape[-1])
    angle = positions.astype(jnp.float32)[:, None] * freq[None, :]
    cosine = jnp.concatenate([jnp.cos(angle), jnp.cos(angle)], axis=-1)[:, None, :]
    sine = jnp.concatenate([jnp.sin(angle), jnp.sin(angle)], axis=-1)[:, None, :]
    turned = jnp.concatenate([-values[..., half:], values[..., :half]], axis=-1)
    return values * cosine + turned * sine


def featurize(projected, features, positions):
    heads = features.shape[0]
    head_size = features.shape[1]
    blocks = projected.reshape(projected.shape[0], heads, 3, head_size)
    factor = head_size ** (-0.25)
    query = rotate(blocks[:, :, 0], positions) * factor
    keyed = rotate(blocks[:, :, 1], positions) * factor
    map_q = (
        jax.nn.elu(jnp.einsum("ghe,hef->ghf", query, features, precision=lax.Precision.HIGHEST))
        + 1.0
    )
    map_k = (
        jax.nn.elu(jnp.einsum("ghe,hef->ghf", keyed, features, precision=lax.Precision.HIGHEST))
        + 1.0
    )
    return (map_q, map_k, blocks[:, :, 2])


def core(map_q, map_k, column_block, key_mask, molecules):
    total_rows, heads, feats = map_q.shape
    head_size = column_block.shape[-1]
    span = total_rows // molecules
    query_maps = map_q.reshape(molecules, span, heads, feats)
    key_maps = (map_k * key_mask[:, None, None]).reshape(molecules, span, heads, feats)
    values_four = column_block.reshape(molecules, span, heads, head_size)
    state = jnp.einsum("mlhf,mlhe->mhfe", key_maps, values_four, precision=lax.Precision.HIGHEST)
    summed = jnp.sum(key_maps, axis=1)
    numer = jnp.einsum("mlhf,mhfe->mlhe", query_maps, state, precision=lax.Precision.HIGHEST)
    denom = jnp.einsum("mlhf,mhf->mlh", query_maps, summed, precision=lax.Precision.HIGHEST)
    return (numer / denom[..., None]).reshape(total_rows, heads * head_size)


def gelu_exact(argument):
    return jax.nn.gelu(argument, approximate=False)


def contract_last(left, right):
    return lax.dot_general(
        left, right, (((1,), (1,)), ((), ())), preferred_element_type=jnp.float32
    )


def contract_first(left, right):
    return lax.dot_general(
        left, right, (((0,), (0,)), ((), ())), preferred_element_type=jnp.float32
    )


def slot_masks(counts):
    slot_index = jnp.arange(MAXLEN, dtype=jnp.int32)
    number = counts.shape[0]
    mask_rows = (slot_index[None, :] < counts[:, None]).astype(jnp.float32).reshape(number * MAXLEN)
    return (mask_rows, jnp.tile(slot_index, number))


def local(
    layer_input,
    lengths,
    ln1_gain,
    ln1_bias,
    w_qkv,
    b_qkv,
    features,
    w_out,
    b_out,
    ln2_gain,
    ln2_bias,
    w_up,
    b_up,
    w_down,
    b_down,
    cotangent,
):
    inputs = layer_input.astype(jnp.float32)
    normed_one, hat_one, factor_one = norm_rows(inputs, ln1_gain, ln1_bias)
    first_local = normed_one.astype(jnp.bfloat16)
    qkv_matrix, out_matrix, qkv_bias, feature_set = (w_qkv, w_out, b_qkv, features)
    attn_mask, attn_positions = slot_masks(lengths)
    attn_molecules = lengths.shape[0]
    first_rows = lax.all_gather(first_local, "mp", axis=0, tiled=True)
    projected = jnp.dot(first_rows, qkv_matrix, preferred_element_type=jnp.float32) + qkv_bias
    feature_out, feature_pull = jax.vjp(
        lambda argument: featurize(argument, feature_set, attn_positions), projected
    )
    widened = tuple((member.astype(jnp.bfloat16).astype(jnp.float32) for member in feature_out))
    attended, core_pull = jax.vjp(
        lambda query_map, key_map, column_block: core(
            query_map, key_map, column_block, attn_mask, attn_molecules
        ),
        *widened
    )
    mixed = attended.astype(jnp.bfloat16)
    middle = (
        inputs
        + lax.psum_scatter(
            jnp.dot(mixed, w_out, preferred_element_type=jnp.float32).astype(jnp.bfloat16),
            "mp",
            scatter_dimension=0,
            tiled=True,
        ).astype(jnp.float32)
        + b_out
    )
    normed_two, hat_two, factor_two = norm_rows(middle, ln2_gain, ln2_bias)
    second = normed_two.astype(jnp.bfloat16)
    second_rows = lax.all_gather(second, "mp", axis=0, tiled=True)
    pre_act = jnp.dot(second_rows, w_up, preferred_element_type=jnp.float32) + b_up
    activated, gelu_pull = jax.vjp(gelu_exact, pre_act)
    hidden = activated.astype(jnp.bfloat16)
    ffn_branch = (
        lax.psum_scatter(
            jnp.dot(hidden, w_down, preferred_element_type=jnp.float32).astype(jnp.bfloat16),
            "mp",
            scatter_dimension=0,
            tiled=True,
        ).astype(jnp.float32)
        + b_down
    )
    outputs = (middle + ffn_branch).astype(jnp.bfloat16)
    grad_output = cotangent.astype(jnp.float32)
    grad_b_down = jnp.sum(grad_output, axis=0)
    grad_rows = lax.all_gather(cotangent, "mp", axis=0, tiled=True)
    grad_hidden = contract_last(grad_rows, w_down)
    grad_pre = gelu_pull(grad_hidden)[0].astype(jnp.bfloat16)
    grad_w_down = contract_first(hidden, grad_rows)
    grad_w_up = contract_first(second_rows, grad_pre)
    grad_b_up = jnp.sum(grad_pre.astype(jnp.float32), axis=0)
    grad_second = lax.psum_scatter(
        contract_last(grad_pre, w_up).astype(jnp.bfloat16), "mp", scatter_dimension=0, tiled=True
    ).astype(jnp.float32)
    grad_mid_norm, grad_ln2_gain, grad_ln2_bias = norm_back(
        grad_second, hat_two, factor_two, ln2_gain
    )
    grad_middle = grad_output + grad_mid_norm
    grad_branch = grad_middle.astype(jnp.bfloat16)
    grad_b_out = jnp.sum(grad_branch.astype(jnp.float32), axis=0)
    branch_rows = lax.all_gather(grad_branch, "mp", axis=0, tiled=True)
    grad_mixed = contract_last(branch_rows, out_matrix)
    out_part = contract_first(mixed, branch_rows)
    grad_maps = core_pull(grad_mixed)
    grad_projected = feature_pull(grad_maps)[0].astype(jnp.bfloat16)
    qkv_bias_part = jnp.sum(grad_projected.astype(jnp.float32), axis=0)
    qkv_part = contract_first(first_rows, grad_projected)
    grad_w_qkv, grad_b_qkv, grad_w_out = (qkv_part, qkv_bias_part, out_part)
    grad_first = lax.psum_scatter(
        contract_last(grad_projected, w_qkv).astype(jnp.bfloat16),
        "mp",
        scatter_dimension=0,
        tiled=True,
    ).astype(jnp.float32)
    grad_in_norm, grad_ln1_gain, grad_ln1_bias = norm_back(
        grad_first, hat_one, factor_one, ln1_gain
    )
    grad_inputs = grad_middle + grad_in_norm
    grad_w_qkv, grad_w_out, grad_w_up, grad_w_down = (
        lax.psum_scatter(grad_w_qkv, "dp", scatter_dimension=0, tiled=True),
        lax.psum_scatter(grad_w_out, "dp", scatter_dimension=1, tiled=True),
        lax.psum_scatter(grad_w_up, "dp", scatter_dimension=0, tiled=True),
        lax.psum_scatter(grad_w_down, "dp", scatter_dimension=1, tiled=True),
    )
    grad_b_qkv, grad_b_up = lax.psum((grad_b_qkv, grad_b_up), "dp")
    summed_small = lax.psum(
        (grad_ln1_gain, grad_ln1_bias, grad_b_out, grad_ln2_gain, grad_ln2_bias, grad_b_down),
        ("dp", "mp"),
    )
    return (
        outputs,
        grad_inputs,
        summed_small[0],
        summed_small[1],
        grad_w_qkv,
        grad_b_qkv,
        grad_w_out,
        summed_small[2],
        summed_small[3],
        summed_small[4],
        grad_w_up,
        grad_b_up,
        grad_w_down,
        summed_small[5],
    )


def solution(mesh):
    placed = (
        P(("dp", "mp"), None),
        P("dp"),
        P(),
        P(),
        P(None, "mp"),
        P("mp"),
        P("mp", None, None),
        P("mp", None),
        P(),
        P(),
        P(),
        P(None, "mp"),
        P("mp"),
        P("mp", None),
        P(),
        P(("dp", "mp"), None),
    )
    return jax.shard_map(
        local,
        mesh=mesh,
        in_specs=placed,
        out_specs=(
            P(("dp", "mp"), None),
            P(("dp", "mp"), None),
            P(),
            P(),
            P("dp", "mp"),
            P("mp"),
            P("mp", "dp"),
            P(),
            P(),
            P(),
            P("dp", "mp"),
            P("mp"),
            P("mp", "dp"),
            P(),
        ),
        check_vma=False,
    )
```

profile of v0, /device:TPU:0, one launch (start us, length us, event | category | flops | bytes accessed | tf_op | source)
XLA Modules:
  0.0 409.1 jit_solution(9099996804335391851)
XLA Ops:
  7.2 1.2 convert_reduce_fusion.4
  8.4 1.2 fusion.46
  9.7 1.9 fusion.91
  14.7 31.8 %all-gather.9.cloned.1.call-done = bf16[4,202,768]{2,1,0:T(8,128)(2,1)} async-done(((bf16[1,202,768]{2,1,0:T(8,128)(2,1)}), bf16[4,202,768]{2,1,0:T(8,128)(2,1)}) %all-gather.9.cloned.1.call-update) | async-done | bytes 1241104 | tf_op jit(solution)/shard_map/all_gather | solution.py:116
  46.5 1.6 reshape.154
  48.1 2.7 convolution_add_fusion
  51.8 1.3 convert_element_type.128
  53.2 1.0 copy_bitcast_fusion
  54.2 1.6 fusion.72
  55.8 1.8 reshape.147
  57.6 1.1 slice_negate_fusion.3
  58.7 1.6 convert_multiply_fusion.4
  60.3 1.3 reshape.146
  61.9 1.1 fusion.98
  63.6 2.4 divide_convert_fusion
  66.6 1.6 convolution_convert_fusion.2
  68.3 32.9 %fusion = bf16[208,768]{1,0:T(8,128)(2,1)} fusion(bf16[808,768]{1,0:T(8,128)(2,1)S(1)} %convolution_convert_fusion.2), kind=kCustom, calls=%all-reduce-scatter | all-reduce-scatter fusion | flops 638977 | bytes 1561088
  101.9 1.3 collective-permute-start
  104.8 2.0 concatenate.18
  107.4 1.7 fusion.90
  109.4 2.7 reshape.158
  112.1 30.2 %all-gather.11.cloned.1.call-done = bf16[4,202,768]{2,1,0:T(8,128)(2,1)} async-done(((bf16[1,202,768]{2,1,0:T(8,128)(2,1)}), bf16[4,202,768]{2,1,0:T(8,128)(2,1)}) %all-gather.11.cloned.1.call-update) | async-done | bytes 1241104 | tf_op jit(solution)/shard_map/all_gather | solution.py:141
  142.3 1.6 reshape.156
  144.0 2.9 fusion.115
  146.9 8.4 %convert_reduce_fusion = (f32[768]{0:T(1024)}, bf16[808,768]{1,0:T(8,128)(2,1)S(1)}, f32[808,768]{1,0:T(8,128)}) fusion(f32[808,768]{1,0:T(8,128)S(1)} %fusion.115, f32[768]{0:T(1024)S(1)} %copy-done.41, bf16[808,768]{1,0:T(8,128)(2,1)S(1)} %copy-done.13, bf16[768,768]{1,0:T(8,128)(2,1)S(1)} %copy-done), kind=kOutput, calls=%fused_computation.2 | convolution fusion | flops 999695616 | bytes 8632320 | tf_op jit(solution)/shard_map/dot_general | solution.py:74
  155.3 1.0 copy-done.47
  156.4 2.3 convolution_convert_fusion
  158.7 28.5 %fusion.2 = bf16[208,768]{1,0:T(8,128)(2,1)S(1)} fusion(bf16[808,768]{1,0:T(8,128)(2,1)} %convolution_convert_fusion), kind=kCustom, calls=%all-reduce-scatter.2 | all-reduce-scatter fusion | flops 638977 | bytes 1561088
  187.3 1.6 collective-permute-start.2
  188.9 1.6 collective-permute-done.2
  190.9 1.1 fusion.52
  192.1 2.1 convert_reduce_fusion.6
  195.1 31.9 %all-gather.15.cloned.1.call-done = bf16[4,202,768]{2,1,0:T(8,128)(2,1)} async-done(((bf16[1,202,768]{2,1,0:T(8,128)(2,1)}), bf16[4,202,768]{2,1,0:T(8,128)(2,1)}) %all-gather.15.cloned.1.call-update) | async-done | bytes 1241104 | tf_op jit(solution)/shard_map/all_gather | solution.py:172
  227.0 1.6 reshape.160
  228.7 2.6 convolution_bitcast_fusion
  231.4 2.9 multiply_convert_fusion
  234.3 1.1 copy-done.10
  235.4 2.9 fusion.119
  238.3 1.5 copy.85
  240.5 4.6 %fusion.118 = f32[768,768]{1,0:T(8,128)} fusion(bf16[808,768]{1,0:T(8,128)(2,1)} %copy-done.12, bf16[808,768]{1,0:T(8,128)(2,1)} %copy-done.47), kind=kOutput, calls=%fused_computation.196 | convolution fusion | flops 953155584 | bytes 4841472 | tf_op jit(solution)/shard_map/dot_general | solution.py:80
  245.4 2.5 fusion.116
  247.8 1.8 reshape.148
  249.6 1.4 multiply_reduce_fusion
  251.8 1.0 copy.86
  252.8 2.0 reshape.151
  254.8 1.2 fusion.96
  256.0 1.5 fusion.19
  258.4 1.0 reshape.150
  259.4 1.7 convolution_bitcast_fusion.1
  262.2 1.9 fusion.59
  264.2 1.9 fusion.61
  267.5 1.0 copy-done.15
  268.5 2.7 fusion.117
  271.3 2.2 convolution_convert_fusion.1
  273.5 2.3 convolution_convert_fusion.3
  275.8 47.7 %fusion.110 = (bf16[208,768]{1,0:T(8,128)(2,1)S(1)}, bf16[208,768]{1,0:T(8,128)(2,1)S(1)}) fusion(bf16[808,768]{1,0:T(8,128)(2,1)} %convolution_convert_fusion.1, bf16[808,768]{1,0:T(8,128)(2,1)} %convolution_convert_fusion.3), kind=kCustom, calls=%all-reduce-scatter.4 | all-reduce-scatter fusion | flops 1277953 | bytes 3121664
  323.6 2.6 collective-permute-start.3
  326.8 2.6 collective-permute-start.1
  329.6 13.6 %all-reduce.16 = (f32[576]{0:T(1024)}, f32[768]{0:T(1024)}) all-reduce(f32[576]{0:T(1024)S(1)} %reduce_sum.181, f32[768]{0:T(1024)S(1)} %copy-done.42), channel_id=1, replica_groups=mesh['dp'=8,'mp'=4] {'dp'}, use_global_device_ids=true, to_apply=%region_20.21 | all-reduce | flops 1344 | bytes 10752 | tf_op jit(solution)/shard_map/psum | solution.py:196
  343.5 1.2 concatenate.19
  345.2 38.1 %all-reduce.15 = (f32[768]{0:T(1024)}, f32[768]{0:T(1024)}, f32[768]{0:T(1024)}, f32[768]{0:T(1024)}, f32[768]{0:T(1024)}, /*index=5*/f32[768]{0:T(1024)}) all-reduce(f32[768]{0:T(1024)S(1)} %get-tuple-element.16, f32[768]{0:T(1024)S(1)} %get-tuple-element.21, ...), channel_id=1, replica_groups=mesh['dp'=8,'mp'=4] {'dp','mp'}, use_global_device_ids=true, to_apply=%region_15.16 | all-reduce | flops 4608 | bytes 36864 | tf_op jit(solution)/shard_map/psum | solution.py:197
  383.3 2.1 fusion.45
  385.4 1.6 copy.94
  387.1 15.2 %reduce-scatter.15.cloned.1.call-done = f32[96,576]{1,0:T(8,128)} async-done(((f32[768,576]{1,0:T(8,128)}), f32[96,576]{1,0:T(8,128)}) %reduce-scatter.15.cloned.1.call-update) | async-done | bytes 221200 | tf_op jit(solution)/shard_map/reduce_scatter | solution.py:191
  (168 shorter events, 16.0 us)
Async XLA Ops:
  7.2 139.7 %copy-start = (bf16[768,768]{1,0:T(8,128)(2,1)S(1)}, bf16[768,768]{1,0:T(8,128)(2,1)}, u32[]{:S(2)}) copy-start(bf16[768,768]{1,0:T(8,128)(2,1)} %param.29) | copy-start | bytes 3538948
  7.2 39.3 %all-gather.9.cloned.1.call-start = ((), (), s32[]{:S(2)}) async-start(), calls=%async_computation.7 | async-start | bytes 1597440 | tf_op jit(solution)/shard_map/all_gather | solution.py:116
  8.4 4.9 %copy-start.29 = (f32[202]{0:T(256)}, f32[202]{0:T(256)S(1)}, u32[]{:S(2)}) copy-start(f32[202]{0:T(256)S(1)} %broadcast_multiply_fusion.7) | copy-start | bytes 2428
  9.7 3.6 copy-start.33
  9.7 38.5 %copy-start.46 = (f32[576]{0:T(1024)S(1)}, f32[576]{0:T(1024)}, u32[]{:S(2)}) copy-start(f32[576]{0:T(1024)} %param.21) | copy-start | bytes 6916
  11.7 97.7 %all-gather.13.cloned.1.call-start = ((), (), s32[]{:S(2)}) async-start(), calls=%async_computation.9 | async-start | bytes 1597440 | tf_op jit(solution)/shard_map/all_gather | solution.py:157
  12.4 129.9 %all-gather.11.cloned.1.call-start = ((), (), s32[]{:S(2)}) async-start(), calls=%async_computation.8 | async-start | bytes 1597440 | tf_op jit(solution)/shard_map/all_gather | solution.py:141
  13.3 45.4 %copy-start.27 = (f32[808]{0:T(1024)}, f32[808]{0:T(1024)S(1)}, u32[]{:S(2)}) copy-start(f32[808]{0:T(1024)S(1)} %reshape.152) | copy-start | bytes 9700
  48.1 2.8 copy-start.8
  51.8 2.4 copy-start.19
  53.1 9.9 %copy-start.4 = (bf16[4,202,3,64]{1,0,3,2:T(4,128)(2,1)}, bf16[4,202,3,64]{1,0,3,2:T(4,128)(2,1)S(1)}, u32[]{:S(2)}) copy-start(bf16[4,202,3,64]{1,0,3,2:T(4,128)(2,1)S(1)} %convert_element_type.128) | copy-start | bytes 930820
  61.8 4.1 %copy-start.21 = (f32[4,3,32]{0,2,1:T(8,128)}, f32[4,3,32]{0,2,1:T(8,128)S(1)}, u32[]{:S(2)}) copy-start(f32[4,3,32]{0,2,1:T(8,128)S(1)} %reduce_sum.170) | copy-start | bytes 4612
  63.1 2.9 copy-start.36
  63.5 2.4 copy-start.22
  66.0 37.2 %copy-start.43 = (u32[32]{0:T(128)S(1)}, u32[32]{0:T(128)}, u32[]{:S(2)}) copy-start(u32[32]{0:T(128)} %constant.120) | copy-start | bytes 388
  66.3 40.5 %copy-start.1 = (bf16[202,768]{1,0:T(8,128)(2,1)S(1)}, bf16[202,768]{1,0:T(8,128)(2,1)}, u32[]{:S(2)}) copy-start(bf16[202,768]{1,0:T(8,128)(2,1)} %param.16) | copy-start | bytes 930820
  66.3 40.5 %copy-start.24 = (f32[768]{0:T(1024)S(1)}, f32[768]{0:T(1024)}, u32[]{:S(2)}) copy-start(f32[768]{0:T(1024)} %param.24) | copy-start | bytes 9220
  66.6 37.8 %copy-start.6 = (bf16[808,192]{0,1:T(8,128)(2,1)}, bf16[808,192]{0,1:T(8,128)(2,1)S(1)}, u32[]{:S(2)}) copy-start(bf16[808,192]{0,1:T(8,128)(2,1)S(1)} %convert_element_type.131) | copy-start | bytes 930820
  101.9 2.9 collective-permute-start
  107.0 5.0 %copy-start.31 = (f32[202]{0:T(256)}, f32[202]{0:T(256)S(1)}, u32[]{:S(2)}) copy-start(f32[202]{0:T(256)S(1)} %broadcast_multiply_fusion.6) | copy-start | bytes 2428
  107.4 4.7 %copy-start.38 = (f32[202]{0:T(256)}, f32[202]{0:T(256)S(1)}, u32[]{:S(2)}) copy-start(f32[202]{0:T(256)S(1)} %add_rsqrt_fusion) | copy-start | bytes 2428
  109.1 117.9 %all-gather.15.cloned.1.call-start = ((), (), s32[]{:S(2)}) async-start(), calls=%async_computation.10 | async-start | bytes 1597440 | tf_op jit(solution)/shard_map/all_gather | solution.py:172
  143.9 2.9 copy-start.12
  143.9 2.9 copy-start.13
  143.9 2.9 copy-start.41
  146.9 8.4 %copy-start.7 = (f32[808,768]{1,0:T(8,128)}, f32[808,768]{1,0:T(8,128)S(1)}, u32[]{:S(2)}) copy-start(f32[808,768]{1,0:T(8,128)S(1)} %fusion.115) | copy-start | bytes 7446532
  146.9 9.5 %copy-start.44 = (bf16[768,768]{1,0:T(8,128)(2,1)S(1)}, bf16[768,768]{1,0:T(8,128)(2,1)}, u32[]{:S(2)}) copy-start(bf16[768,768]{1,0:T(8,128)(2,1)} %param.27) | copy-start | bytes 3538948
  155.3 1.1 copy-start.47
  156.4 34.5 %copy-start.25 = (f32[768]{0:T(1024)S(1)}, f32[768]{0:T(1024)}, u32[]{:S(2)}) copy-start(f32[768]{0:T(1024)} %param.25) | copy-start | bytes 9220
  156.4 34.5 %copy-start.32 = (f32[202]{0:T(256)S(1)}, f32[202]{0:T(256)}, u32[]{:S(2)}) copy-start(f32[202]{0:T(256)} %copy-done.31) | copy-start | bytes 2428
  156.4 34.6 %copy-start.39 = (f32[202]{0:T(256)S(1)}, f32[202]{0:T(256)}, u32[]{:S(2)}) copy-start(f32[202]{0:T(256)} %copy-done.38) | copy-start | bytes 2428
  187.3 3.2 collective-permute-start.2
  194.2 0.9 copy-start.2
  195.0 190.4 %reduce-scatter.21.cloned.1.call-start = ((), (), s32[]{:S(2)}) async-start(), calls=%async_computation.11 | async-start | bytes 884736
  231.3 155.8 %reduce-scatter.19.cloned.1.call-start = ((), (), s32[]{:S(2)}) async-start(), calls=%async_computation.6 | async-start | bytes 2654208 | tf_op jit(solution)/shard_map/reduce_scatter | solution.py:194
  231.4 4.0 copy-start.14
  234.3 1.1 copy-start.10
  238.3 148.8 %reduce-scatter.17.cloned.1.call-start = ((), (), s32[]{:S(2)}) async-start(), calls=%async_computation.5 | async-start | bytes 2654208 | tf_op jit(solution)/shard_map/reduce_scatter | solution.py:193
  245.1 6.0 %copy-start.40 = (f32[4,3,32]{2,1,0:T(4,128)S(1)}, f32[4,3,32]{2,1,0:T(4,128)}, u32[]{:S(2)}) copy-start(f32[4,3,32]{2,1,0:T(4,128)} %copy.85) | copy-start | bytes 4612
  245.1 157.2 %reduce-scatter.15.cloned.1.call-start = ((), (), s32[]{:S(2)}) async-start(), calls=%async_computation.4 | async-start | bytes 2211840 | tf_op jit(solution)/shard_map/reduce_scatter | solution.py:191
  247.8 3.3 copy-start.23
  247.8 3.3 copy-start.37
  251.8 5.7 %copy-start.5 = (bf16[4,202,3,64]{1,0,3,2:T(4,128)(2,1)S(1)}, bf16[4,202,3,64]{1,0,3,2:T(4,128)(2,1)}, u32[]{:S(2)}) copy-start(bf16[4,202,3,64]{1,0,3,2:T(4,128)(2,1)} %copy-done.4) | copy-start | bytes 930820
  257.5 0.7 copy-start.20
  261.2 3.0 copy-start.28
  262.2 3.8 copy-start.17
  266.1 0.9 copy-start.18
  267.2 1.4 copy-start.9
  267.5 1.0 copy-start.15
  268.5 2.8 copy-start.11
  271.3 2.2 copy-start.16
  271.3 2.2 copy-start.45
  275.8 53.8 %copy-start.42 = (f32[768]{0:T(1024)S(1)}, f32[768]{0:T(1024)}, u32[]{:S(2)}) copy-start(f32[768]{0:T(1024)} %get-tuple-element.34) | copy-start | bytes 9220
  275.8 68.9 %copy-start.26 = (f32[768]{0:T(1024)S(1)}, f32[768]{0:T(1024)}, u32[]{:S(2)}) copy-start(f32[768]{0:T(1024)} %param.18) | copy-start | bytes 9220
  275.8 68.9 %copy-start.30 = (f32[202]{0:T(256)S(1)}, f32[202]{0:T(256)}, u32[]{:S(2)}) copy-start(f32[202]{0:T(256)} %copy-done.29) | copy-start | bytes 2428
  275.8 68.9 %copy-start.34 = (f32[202]{0:T(256)S(1)}, f32[202]{0:T(256)}, u32[]{:S(2)}) copy-start(f32[202]{0:T(256)} %copy-done.33) | copy-start | bytes 2428
  275.8 69.4 %copy-start.35 = (f32[768]{0:T(1024)S(1)}, f32[768]{0:T(1024)}, u32[]{:S(2)}) copy-start(f32[768]{0:T(1024)} %get-tuple-element.14) | copy-start | bytes 9220
  275.8 107.5 %copy-start.3 = (f32[202,768]{1,0:T(8,128)S(1)}, f32[202,768]{1,0:T(8,128)}, u32[]{:S(2)}) copy-start(f32[202,768]{1,0:T(8,128)} %copy-done.2) | copy-start | bytes 1861636
  323.6 19.5 %collective-permute-start.3 = (bf16[18,768]{1,0:T(8,128)(2,1)S(1)}, bf16[18,768]{1,0:T(8,128)(2,1)S(1)}, u32[]{:S(2)}, u32[]{:S(2)}) collective-permute-start(bf16[18,768]{1,0:T(8,128)(2,1)S(1)} %slice.39), channel_id=1, source_target_pairs={{0,1},{1,2},{2,3},{4,5},{5,6},{6,7},{8,9},{9,10},{10,11},{12,13},{... | collective-permute-start | bytes 82952
  326.8 16.7 %collective-permute-start.1 = (bf16[18,768]{1,0:T(8,128)(2,1)}, bf16[18,768]{1,0:T(8,128)(2,1)}, u32[]{:S(2)}, u32[]{:S(2)}) collective-permute-start(bf16[18,768]{1,0:T(8,128)(2,1)} %slice.37), channel_id=1, source_target_pairs={{0,1},{1,2},{2,3},{4,5},{5,6},{6,7},{8,9},{9,10},{10,11},{12,13},{... | collective-permute-start | bytes 82952
Sparse Core Ops, SparseCore 0:
  11.8 34.6 all-gather.8
  48.1 36.3 all-gather.12
  109.2 33.0 all-gather.10
  195.1 31.8 all-gather.14
  231.4 34.0 reduce-scatter.20
  269.3 42.3 reduce-scatter.18
  315.6 42.4 reduce-scatter.16
  362.1 40.1 reduce-scatter.14
where the time goes:
time: 411 us; the launch traced here: 409 us
  blocking collectives  161 us (39%)
  waiting for transfers between devices  112 us (27%)
  matrix products  54.1 us (13%)
  local copies, waits for them, and re-layouts  35.5 us (9%)
  other arithmetic  22.2 us (5%)
  between operations  15.7 us (4%)
  starting transfers between devices  8.88 us (2%)
    unnamed x3, blocking collectives  109 us
    psum x1, blocking collectives, local(): lax.psum((grad_ln1_gain, grad_ln1_bias, grad_b_out, grad_ln2_gain, grad_l...  38.1 us
    all_gather x1, waiting for transfers between devices, local(): branch_rows = lax.all_gather(grad_branch, 'mp', axis=0, tiled=True)  31.9 us
    all_gather x1, waiting for transfers between devices, local(): first_rows = lax.all_gather(first_local, 'mp', axis=0, tiled=True)  31.8 us
    all_gather x1, waiting for transfers between devices, local(): second_rows = lax.all_gather(second, 'mp', axis=0, tiled=True)  30.2 us
    unnamed x111, local copies, waits for them, and re-layouts  20.4 us
    dot_general x4, matrix products, contract_last(): lax.dot_general(left, right, (((1,), (1,)), ((), ())), preferred_element_...  15.5 us
    reduce_scatter x1, waiting for transfers between devices, local(): lax.psum_scatter(grad_w_qkv, 'dp', scatter_dimension=0, tiled=True)  15.2 us
  transfers between devices with their start and end apart: 12, of which 6 were waited for; matrix products, arithmetic and copies ran while one was open for 39% of the time, Pallas kernels for 0%

commit v1 on v0

--- a/solution.py
+++ b/solution.py
@@ -5,6 +5,23 @@
 
 MAXLEN = 202
 EPSILON = 1e-05
+
+
+def joined_along(blocks, dim):
+    blocks = jnp.moveaxis(blocks, 0, dim)
+    shape = blocks.shape
+    return blocks.reshape(*shape[:dim], shape[dim] * shape[dim + 1], *shape[dim + 2 :])
+
+
+def doubled(x, axis):
+    size, mine = (lax.axis_size(axis), lax.axis_index(axis))
+    parts, stride = (x[None], 1)
+    while stride < size:
+        other = lax.ppermute(parts, axis, [(i, i ^ stride) for i in range(size)])
+        low = mine & stride == 0
+        parts = jnp.concatenate([jnp.where(low, parts, other), jnp.where(low, other, parts)])
+        stride *= 2
+    return parts
 
 
 def norm_rows(values, gain, shift):
@@ -169,7 +186,7 @@
     grad_middle = grad_output + grad_mid_norm
     grad_branch = grad_middle.astype(jnp.bfloat16)
     grad_b_out = jnp.sum(grad_branch.astype(jnp.float32), axis=0)
-    branch_rows = lax.all_gather(grad_branch, "mp", axis=0, tiled=True)
+    branch_rows = joined_along(doubled(grad_branch, "mp"), 0)
     grad_mixed = contract_last(branch_rows, out_matrix)
     out_part = contract_first(mixed, branch_rows)
     grad_maps = core_pull(grad_mixed)

time: 411 us -> 418 us (1.017)
    all_gather x1 -> x0, waiting for transfers between devices: 31.9 us -> none  [local(): branch_rows = lax.all_gather(grad_branch, 'mp', axis=0, tiled=True)]
    ppermute x0 -> x2, waiting for transfers between devices: none -> 30.8 us  [doubled(): other = lax.ppermute(parts, axis, [(i, i ^ stride) for i in range(size)])]
    unnamed x111 -> x116, local copies, waits for them, and re-layouts: 20.4 us -> 20.7 us
  transfers between devices with their start and end apart: 12 -> 13, of which waited for: 6 -> 7; matrix products, arithmetic and copies ran while one was open for 39% -> 37% of each run, Pallas kernels for 0% -> 0%
where the time goes in v1:
time: 418 us; the launch traced here: 417 us
  blocking collectives  162 us (39%)
  waiting for transfers between devices  114 us (27%)
  matrix products  52.4 us (13%)
  local copies, waits for them, and re-layouts  36.8 us (9%)
  other arithmetic  23.8 us (6%)
  between operations  15.7 us (4%)
  starting transfers between devices  12.2 us (3%)
    unnamed x3, blocking collectives  110 us
    psum x1, blocking collectives, local(): lax.psum((grad_ln1_gain, grad_ln1_bias, grad_b_out, grad_ln2_gain, grad_l...  38.2 us
    all_gather x1, waiting for transfers between devices, local(): first_rows = lax.all_gather(first_local, 'mp', axis=0, tiled=True)  31.8 us
    ppermute x2, waiting for transfers between devices, doubled(): other = lax.ppermute(parts, axis, [(i, i ^ stride) for i in range(size)])  30.8 us
    all_gather x1, waiting for transfers between devices, local(): second_rows = lax.all_gather(second, 'mp', axis=0, tiled=True)  30.3 us
    unnamed x116, local copies, waits for them, and re-layouts  20.7 us
    reduce_scatter x1, waiting for transfers between devices, local(): lax.psum_scatter(grad_w_qkv, 'dp', scatter_dimension=0, tiled=True)  18.7 us
    dot_general x4, matrix products, contract_last(): lax.dot_general(left, right, (((1,), (1,)), ((), ())), preferred_element_...  14.9 us
  transfers between devices with their start and end apart: 13, of which 7 were waited for; matrix products, arithmetic and copies ran while one was open for 37% of the time, Pallas kernels for 0%

profile of v1, /device:TPU:0, one launch (start us, length us, event | category | flops | bytes accessed | tf_op | source)
XLA Modules:
  0.0 417.0 jit_solution(10652201061867154993)
XLA Ops:
  7.2 1.2 convert_reduce_fusion.4
  8.4 1.2 fusion.45
  9.7 1.9 fusion.90
  14.7 31.8 %all-gather.7.cloned.1.call-done = bf16[4,202,768]{2,1,0:T(8,128)(2,1)} async-done(((bf16[1,202,768]{2,1,0:T(8,128)(2,1)}), bf16[4,202,768]{2,1,0:T(8,128)(2,1)}) %all-gather.7.cloned.1.call-update) | async-done | bytes 1241104 | tf_op jit(solution)/shard_map/all_gather | solution.py:133
  46.5 2.7 reshape.159
  49.2 2.7 convolution_add_fusion
  52.7 1.3 convert_element_type.129
  54.1 1.0 copy_bitcast_fusion
  55.2 1.6 fusion.71
  56.7 1.1 reshape.152
  57.8 1.2 slice_negate_fusion.3
  59.1 1.6 convert_multiply_fusion.4
  60.7 1.3 reshape.151
  63.0 1.4 divide_convert_fusion
  65.1 1.6 convolution_convert_fusion.2
  66.7 33.8 %fusion = bf16[208,768]{1,0:T(8,128)(2,1)S(1)} fusion(bf16[808,768]{1,0:T(8,128)(2,1)} %convolution_convert_fusion.2), kind=kCustom, calls=%all-reduce-scatter | all-reduce-scatter fusion | flops 638977 | bytes 1561088
  100.5 1.3 collective-permute-start.2
  105.7 2.7 reshape.163
  108.4 30.3 %all-gather.9.cloned.1.call-done = bf16[4,202,768]{2,1,0:T(8,128)(2,1)} async-done(((bf16[1,202,768]{2,1,0:T(8,128)(2,1)}), bf16[4,202,768]{2,1,0:T(8,128)(2,1)}) %all-gather.9.cloned.1.call-update) | async-done | bytes 1241104 | tf_op jit(solution)/shard_map/all_gather | solution.py:158
  138.6 2.8 reshape.161
  141.4 2.9 fusion.115
  144.4 8.4 %convert_reduce_fusion = (f32[768]{0:T(1024)}, bf16[808,768]{1,0:T(8,128)(2,1)S(1)}, f32[808,768]{1,0:T(8,128)}) fusion(f32[808,768]{1,0:T(8,128)S(1)} %fusion.115, f32[768]{0:T(1024)S(1)} %copy-done.42, bf16[808,768]{1,0:T(8,128)(2,1)S(1)} %copy-done.13, bf16[768,768]{1,0:T(8,128)(2,1)S(1)} %copy-done), kind=kOutput, calls=%fused_computation.2 | convolution fusion | flops 999695616 | bytes 8632320 | tf_op jit(solution)/shard_map/dot_general | solution.py:91
  152.7 1.1 copy-done.50
  153.8 2.2 convolution_convert_fusion
  156.0 28.6 %fusion.2 = bf16[208,768]{1,0:T(8,128)(2,1)S(1)} fusion(bf16[808,768]{1,0:T(8,128)(2,1)} %convolution_convert_fusion), kind=kCustom, calls=%all-reduce-scatter.2 | all-reduce-scatter fusion | flops 638977 | bytes 1561088
  184.6 1.6 collective-permute-start.4
  186.2 1.6 collective-permute-done.4
  188.2 1.1 fusion.51
  189.3 2.3 convert_reduce_fusion.6
  191.6 2.4 collective-permute-start
  194.0 5.2 %collective-permute-done = bf16[1,202,768]{2,1,0:T(8,128)(2,1)} collective-permute-done((bf16[1,202,768]{2,1,0:T(8,128)(2,1)S(1)}, bf16[1,202,768]{2,1,0:T(8,128)(2,1)}, u32[]{:S(2)}, u32[]{:S(2)}) %collective-permute-start) | collective-permute-done | bytes 310304 | tf_op jit(solution)/shard_map/ppermute | solution.py:20
  199.3 1.0 broadcast_select_fusion.3
  201.1 1.3 copy.77
  202.4 1.6 collective-permute-start.1
  204.0 25.6 %collective-permute-done.1 = bf16[2,202,768]{2,0,1:T(2,128)(2,1)} collective-permute-done((bf16[2,202,768]{2,0,1:T(2,128)(2,1)}, bf16[2,202,768]{2,0,1:T(2,128)(2,1)}, u32[]{:S(2)}, u32[]{:S(2)}) %collective-permute-start.1) | collective-permute-done | bytes 620576 | tf_op jit(solution)/shard_map/ppermute | solution.py:20
  229.6 1.3 broadcast_select_fusion.1
  232.0 1.2 pad_maximum_fusion
  233.2 2.7 reshape.156
  235.8 2.9 convolution_bitcast_fusion
  238.9 2.9 multiply_convert_fusion
  241.8 1.0 copy-done.12
  242.8 2.9 fusion.118
  246.5 4.7 %fusion.117 = f32[768,768]{1,0:T(8,128)} fusion(bf16[808,768]{1,0:T(8,128)(2,1)} %reshape.161, bf16[808,768]{1,0:T(8,128)(2,1)} %copy-done.50), kind=kOutput, calls=%fused_computation.202 | convolution fusion | flops 953155584 | bytes 4841472 | tf_op jit(solution)/shard_map/dot_general | solution.py:97
  251.5 2.0 multiply_reduce_fusion
  254.5 1.0 copy.86
  255.5 2.0 reshape.155
  257.7 1.7 fusion.91
  261.4 1.7 convolution_bitcast_fusion.1
  263.7 1.4 reshape.153
  265.1 1.9 fusion.58
  267.0 1.9 fusion.60
  271.6 2.8 fusion.116
  274.4 3.6 convolution_convert_fusion.1
  277.9 2.3 convolution_convert_fusion.3
  280.2 47.6 %fusion.110 = (bf16[208,768]{1,0:T(8,128)(2,1)S(1)}, bf16[208,768]{1,0:T(8,128)(2,1)S(1)}) fusion(bf16[808,768]{1,0:T(8,128)(2,1)} %convolution_convert_fusion.1, bf16[808,768]{1,0:T(8,128)(2,1)} %convolution_convert_fusion.3), kind=kCustom, calls=%all-reduce-scatter.4 | all-reduce-scatter fusion | flops 1277953 | bytes 3121664
  327.9 1.3 collective-permute-start.5
  329.8 3.3 collective-permute-start.3
  333.2 13.5 %all-reduce.16 = (f32[576]{0:T(1024)}, f32[768]{0:T(1024)}) all-reduce(f32[576]{0:T(1024)S(1)} %reduce_sum.181, f32[768]{0:T(1024)S(1)} %copy-done.44), channel_id=1, replica_groups=mesh['dp'=8,'mp'=4] {'dp'}, use_global_device_ids=true, to_apply=%region_20.21 | all-reduce | flops 1344 | bytes 10752 | tf_op jit(solution)/shard_map/psum | solution.py:213
  347.1 1.2 concatenate.27
  348.2 1.1 fusion.52
  349.4 38.2 %all-reduce.15 = (f32[768]{0:T(1024)}, f32[768]{0:T(1024)}, f32[768]{0:T(1024)}, f32[768]{0:T(1024)}, f32[768]{0:T(1024)}, /*index=5*/f32[768]{0:T(1024)}) all-reduce(f32[768]{0:T(1024)S(1)} %get-tuple-element.16, f32[768]{0:T(1024)S(1)} %get-tuple-element.21, ...), channel_id=1, replica_groups=mesh['dp'=8,'mp'=4] {'dp','mp'}, use_global_device_ids=true, to_apply=%region_15.16 | all-reduce | flops 4608 | bytes 36864 | tf_op jit(solution)/shard_map/psum | solution.py:214
  387.6 2.2 fusion.44
  389.8 1.7 copy.95
  391.4 18.7 %reduce-scatter.15.cloned.1.call-done = f32[96,576]{1,0:T(8,128)} async-done(((f32[768,576]{1,0:T(8,128)}), f32[96,576]{1,0:T(8,128)}) %reduce-scatter.15.cloned.1.call-update) | async-done | bytes 221200 | tf_op jit(solution)/shard_map/reduce_scatter | solution.py:208
  (178 shorter events, 19.5 us)
Async XLA Ops:
  7.2 137.1 %copy-start = (bf16[768,768]{1,0:T(8,128)(2,1)S(1)}, bf16[768,768]{1,0:T(8,128)(2,1)}, u32[]{:S(2)}) copy-start(bf16[768,768]{1,0:T(8,128)(2,1)} %param.29) | copy-start | bytes 3538948
  7.2 39.3 %all-gather.7.cloned.1.call-start = ((), (), s32[]{:S(2)}) async-start(), calls=%async_computation.7 | async-start | bytes 1597440 | tf_op jit(solution)/shard_map/all_gather | solution.py:133
  8.4 4.9 %copy-start.33 = (f32[202]{0:T(256)}, f32[202]{0:T(256)S(1)}, u32[]{:S(2)}) copy-start(f32[202]{0:T(256)S(1)} %broadcast_multiply_fusion.7) | copy-start | bytes 2428
  9.7 3.6 copy-start.36
  9.7 39.5 %copy-start.48 = (f32[576]{0:T(1024)S(1)}, f32[576]{0:T(1024)}, u32[]{:S(2)}) copy-start(f32[576]{0:T(1024)} %param.21) | copy-start | bytes 6916
  11.7 94.1 %all-gather.11.cloned.1.call-start = ((), (), s32[]{:S(2)}) async-start(), calls=%async_computation.9 | async-start | bytes 1597440 | tf_op jit(solution)/shard_map/all_gather | solution.py:174
  12.4 126.2 %all-gather.9.cloned.1.call-start = ((), (), s32[]{:S(2)}) async-start(), calls=%async_computation.8 | async-start | bytes 1597440 | tf_op jit(solution)/shard_map/all_gather | solution.py:158
  13.3 45.8 %copy-start.31 = (f32[808]{0:T(1024)}, f32[808]{0:T(1024)S(1)}, u32[]{:S(2)}) copy-start(f32[808]{0:T(1024)S(1)} %reshape.157) | copy-start | bytes 9700
  52.7 2.4 copy-start.17
  54.1 8.4 %copy-start.2 = (bf16[4,202,3,64]{1,0,3,2:T(4,128)(2,1)}, bf16[4,202,3,64]{1,0,3,2:T(4,128)(2,1)S(1)}, u32[]{:S(2)}) copy-start(bf16[4,202,3,64]{1,0,3,2:T(4,128)(2,1)S(1)} %convert_element_type.129) | copy-start | bytes 930820
  57.8 5.2 %copy-start.18 = (bf16[4,202,3,32]{1,0,3,2:T(4,128)(2,1)}, bf16[4,202,3,32]{1,0,3,2:T(4,128)(2,1)S(1)}, u32[]{:S(2)}) copy-start(bf16[4,202,3,32]{1,0,3,2:T(4,128)(2,1)S(1)} %reshape.152) | copy-start | bytes 465412
  62.2 2.3 copy-start.21
  62.5 2.0 copy-start.27
  62.5 1.9 copy-start.37
  62.5 2.5 copy-start.23
  63.0 3.7 copy-start.24
  64.5 37.4 %copy-start.45 = (u32[32]{0:T(128)S(1)}, u32[32]{0:T(128)}, u32[]{:S(2)}) copy-start(u32[32]{0:T(128)} %constant.130) | copy-start | bytes 388
  64.8 39.0 %copy-start.1 = (bf16[202,768]{1,0:T(8,128)(2,1)S(1)}, bf16[202,768]{1,0:T(8,128)(2,1)}, u32[]{:S(2)}) copy-start(bf16[202,768]{1,0:T(8,128)(2,1)} %param.16) | copy-start | bytes 930820
  64.8 39.0 %copy-start.26 = (f32[768]{0:T(1024)S(1)}, f32[768]{0:T(1024)}, u32[]{:S(2)}) copy-start(f32[768]{0:T(1024)} %param.24) | copy-start | bytes 9220
  65.1 39.3 %copy-start.29 = (f32[768]{0:T(1024)S(1)}, f32[768]{0:T(1024)}, u32[]{:S(2)}) copy-start(f32[768]{0:T(1024)} %param.25) | copy-start | bytes 9220
  65.1 39.3 %copy-start.41 = (f32[768]{0:T(1024)S(1)}, f32[768]{0:T(1024)}, u32[]{:S(2)}) copy-start(f32[768]{0:T(1024)} %param.26) | copy-start | bytes 9220
  100.5 2.9 collective-permute-start.2
  104.1 84.1 %copy-start.35 = (f32[202]{0:T(256)}, f32[202]{0:T(256)S(1)}, u32[]{:S(2)}) copy-start(f32[202]{0:T(256)S(1)} %broadcast_multiply_fusion.6) | copy-start | bytes 2428
  104.4 83.8 %copy-start.40 = (f32[202]{0:T(256)}, f32[202]{0:T(256)S(1)}, u32[]{:S(2)}) copy-start(f32[202]{0:T(256)S(1)} %add_rsqrt_fusion) | copy-start | bytes 2428
  105.5 284.3 %reduce-scatter.21.cloned.1.call-start = ((), (), s32[]{:S(2)}) async-start(), calls=%async_computation.10 | async-start | bytes 884736
  141.4 2.9 copy-start.13
  141.4 2.9 copy-start.42
  144.3 8.4 %copy-start.10 = (f32[808,768]{1,0:T(8,128)}, f32[808,768]{1,0:T(8,128)S(1)}, u32[]{:S(2)}) copy-start(f32[808,768]{1,0:T(8,128)S(1)} %fusion.115) | copy-start | bytes 7446532
  144.3 9.4 %copy-start.46 = (bf16[768,768]{1,0:T(8,128)(2,1)S(1)}, bf16[768,768]{1,0:T(8,128)(2,1)}, u32[]{:S(2)}) copy-start(bf16[768,768]{1,0:T(8,128)(2,1)} %param.27) | copy-start | bytes 3538948
  152.7 1.1 copy-start.50
  184.6 3.2 collective-permute-start.4
  188.2 1.1 copy-start.5
  191.6 7.6 %collective-permute-start = (bf16[1,202,768]{2,1,0:T(8,128)(2,1)S(1)}, bf16[1,202,768]{2,1,0:T(8,128)(2,1)}, u32[]{:S(2)}, u32[]{:S(2)}) collective-permute-start(bf16[1,202,768]{2,1,0:T(8,128)(2,1)S(1)} %convert_bitcast_fusion), channel_id=1, source_target_pairs={{0,1},{1,0},{2,3},{3,2},{4,5},{5,4},{6,7},{7,6},{8,9},{9,8},{10,11... | collective-permute-start | bytes 930824 | tf_op jit(solution)/shard_map/ppermute | solution.py:20
  200.3 0.7 copy-start.4
  202.4 27.2 %collective-permute-start.1 = (bf16[2,202,768]{2,0,1:T(2,128)(2,1)}, bf16[2,202,768]{2,0,1:T(2,128)(2,1)}, u32[]{:S(2)}, u32[]{:S(2)}) collective-permute-start(bf16[2,202,768]{2,0,1:T(2,128)(2,1)} %copy.77), channel_id=1, source_target_pairs={{0,2},{1,3},{2,0},{3,1},{4,6},{5,7},{6,4},{7,5},{8,10},{9,11},{10,... | collective-permute-start | bytes 1861640 | tf_op jit(solution)/shard_map/ppermute | solution.py:20
  230.9 0.9 copy-start.7
  230.9 1.0 copy-start.9
  233.2 5.7 %copy-start.43 = (f32[768]{0:T(1024)S(1)}, f32[768]{0:T(1024)}, u32[]{:S(2)}) copy-start(f32[768]{0:T(1024)} %param.28) | copy-start | bytes 9220
  238.8 152.6 %reduce-scatter.19.cloned.1.call-start = ((), (), s32[]{:S(2)}) async-start(), calls=%async_computation.6 | async-start | bytes 2654208 | tf_op jit(solution)/shard_map/reduce_scatter | solution.py:211
  238.8 3.9 copy-start.14
  241.7 1.0 copy-start.12
  242.8 3.0 copy-start.22
  242.8 3.1 copy-start.28
  245.7 145.7 %reduce-scatter.17.cloned.1.call-start = ((), (), s32[]{:S(2)}) async-start(), calls=%async_computation.5 | async-start | bytes 2654208 | tf_op jit(solution)/shard_map/reduce_scatter | solution.py:210
  246.5 5.0 %copy-start.8 = (bf16[2,202,768]{2,1,0:T(8,128)(2,1)S(1)}, bf16[2,202,768]{2,1,0:T(8,128)(2,1)}, u32[]{:S(2)}) copy-start(bf16[2,202,768]{2,1,0:T(8,128)(2,1)} %copy-done.7) | copy-start | bytes 1861636
  251.2 158.9 %reduce-scatter.15.cloned.1.call-start = ((), (), s32[]{:S(2)}) async-start(), calls=%async_computation.4 | async-start | bytes 2211840 | tf_op jit(solution)/shard_map/reduce_scatter | solution.py:208
  251.5 2.1 copy-start.25
  251.5 2.1 copy-start.38
  253.5 1.0 copy-start.49
  253.5 4.0 copy-start.19
  253.5 4.2 %copy-start.39 = (f32[4,3,1,202]{3,1,0,2:T(4,128)S(1)}, f32[4,3,1,202]{3,1,0,2:T(4,128)}, u32[]{:S(2)}) copy-start(f32[4,3,1,202]{3,1,0,2:T(4,128)} %copy-done.37) | copy-start | bytes 29092
  254.5 5.0 %copy-start.3 = (bf16[4,202,3,64]{1,0,3,2:T(4,128)(2,1)S(1)}, bf16[4,202,3,64]{1,0,3,2:T(4,128)(2,1)}, u32[]{:S(2)}) copy-start(bf16[4,202,3,64]{1,0,3,2:T(4,128)(2,1)} %copy-done.2) | copy-start | bytes 930820
  259.5 0.7 copy-start.20
  263.2 3.8 copy-start.32
  263.7 5.2 %copy-start.15 = (f32[808,64]{0,1:T(8,128)S(1)}, f32[808,64]{0,1:T(8,128)}, u32[]{:S(2)}) copy-start(f32[808,64]{0,1:T(8,128)} %get-tuple-element.64) | copy-start | bytes 620548
  268.9 0.9 copy-start.16
  269.2 1.1 copy-start.6
  270.3 1.3 copy-start.11
  274.4 3.6 copy-start.47
  280.2 53.0 %copy-start.44 = (f32[768]{0:T(1024)S(1)}, f32[768]{0:T(1024)}, u32[]{:S(2)}) copy-start(f32[768]{0:T(1024)} %get-tuple-element.34) | copy-start | bytes 9220
  280.2 68.0 %copy-start.30 = (f32[768]{0:T(1024)S(1)}, f32[768]{0:T(1024)}, u32[]{:S(2)}) copy-start(f32[768]{0:T(1024)} %param.18) | copy-start | bytes 9220
  280.2 68.0 %copy-start.34 = (f32[202]{0:T(256)S(1)}, f32[202]{0:T(256)}, u32[]{:S(2)}) copy-start(f32[202]{0:T(256)} %copy-done.33) | copy-start | bytes 2428
  327.9 18.8 %collective-permute-start.5 = (bf16[18,768]{1,0:T(8,128)(2,1)S(1)}, bf16[18,768]{1,0:T(8,128)(2,1)S(1)}, u32[]{:S(2)}, u32[]{:S(2)}) collective-permute-start(bf16[18,768]{1,0:T(8,128)(2,1)S(1)} %slice.39), channel_id=1, source_target_pairs={{0,1},{1,2},{2,3},{4,5},{5,6},{6,7},{8,9},{9,10},{10,11},{12,13},{... | collective-permute-start | bytes 82952
  329.8 17.2 %collective-permute-start.3 = (bf16[18,768]{1,0:T(8,128)(2,1)}, bf16[18,768]{1,0:T(8,128)(2,1)}, u32[]{:S(2)}, u32[]{:S(2)}) collective-permute-start(bf16[18,768]{1,0:T(8,128)(2,1)} %slice.37), channel_id=1, source_target_pairs={{0,1},{1,2},{2,3},{4,5},{5,6},{6,7},{8,9},{9,10},{10,11},{12,13},{... | collective-permute-start | bytes 82952
Sparse Core Ops, SparseCore 0:
  11.8 34.6 all-gather.6
  48.0 36.9 all-gather.10
  105.6 33.0 all-gather.8
  238.9 34.4 reduce-scatter.20
  277.2 42.3 reduce-scatter.18
  323.3 42.6 reduce-scatter.16
  370.0 40.1 reduce-scatter.14
